TPU v7x, 768 devices: a whole 4x8x12 slice. The times are simulated.
768 devices in a mesh: rows: 64 (over x, y, core), ang: 12 (over z).
Axes of the slice: x: 4, y: 8, z: 12, core: 2. Of those that a mesh axis runs over, the one named last changes fastest.
Arguments:
- delta_obj: float32 [8704, 2, 1536], P('rows', None, 'ang'), may hold values from -4 to 4
- beta_obj: float32 [8704, 2, 1536], P('rows', None, 'ang'), may hold values from 0 to 0.15
- layer_shifts: int32 [12, 2], replicated, may hold values from -8 to 8
- illumination_field: float32 [2, 128, 128], replicated, may hold values from -6 to 6
- amplitudes: float32 [12, 256, 128, 128], P('ang', 'rows'), may hold values from 0.2 to 3
- positions: int32 [12, 256, 2], P('ang', 'rows'), may hold values from 0 to 1408, as said below
- scan_counts: int32 [12, 64], P('ang', 'rows'), may hold values from 1 to 4, as said below
Outputs:
- grad_delta: float32 [8704, 2, 1536], P('rows', None, 'ang')
- grad_beta: float32 [8704, 2, 1536], P('rows', None, 'ang')
Inputs may be any that keep to these rules, and one draw needn't show every extreme that they name: `positions`: within each tile at each angle the slots come in order: a first group, at most 1 of them, has row offsets above 8; all later slots have row offsets of at most 8. Columns are at most 1408. `scan_counts`: slots of a tile from this number on are not used.
All inputs are finite; a program needn't handle non-finite values.
Results may differ from a plain program's by a relative error of at most 0.0046.
Values may be sent and summed in bfloat16 or wider, within the bound.
A program may use at most 32 MiB of HBM per device.

v0:
```python
import functools
import math

import jax
import jax.numpy as jnp
import numpy as np
from jax import lax
from jax.experimental import pallas as pl
from jax.experimental.pallas import tpu as pltpu
from jax.sharding import PartitionSpec as P

PIX = 128
TH = 136
COLS = 128
LAYERS = 2
SHIFT = 8
SLOTS = 4
AMP_FLOOR = 0.1
BLOCK_ROWS = 2 * LAYERS * TH
CHAN_ROWS = LAYERS * TH
F32 = jnp.float32
BF16 = jnp.bfloat16


def dft_constants():
    counter = np.arange(PIX)
    angle = (counter[:, None] * counter[None, :] % PIX) * (2.0 * math.pi / PIX)
    scale = 1.0 / math.sqrt(PIX)
    re = np.cos(angle) * scale
    im = -np.sin(angle) * scale
    m1 = np.block([[re, -im], [im, re]])
    m2 = np.block([[re, im], [-im, re]])

    def split(m):
        hi = m.astype(BF16)
        lo = (m - hi.astype(np.float64)).astype(BF16)
        return np.asarray(hi), np.asarray(lo)

    return split(m1) + split(m2)


def split_f32(x):
    hi = x.astype(BF16)
    lo = (x - hi.astype(F32)).astype(BF16)
    return hi, lo


def dot(a, b):
    return jnp.dot(a, b, preferred_element_type=F32)


def left_product(hi, lo, data):
    d_hi, d_lo = split_f32(data)
    return dot(hi, d_hi) + (dot(hi, d_lo) + dot(lo, d_hi))


def right_product(data, hi, lo):
    d_hi, d_lo = split_f32(data)
    return dot(d_hi, hi) + (dot(d_lo, hi) + dot(d_hi, lo))


def sin_cos(x):
    k = jnp.floor(x * (2.0 / math.pi) + 0.5)
    y = x - k * 1.5703125
    y = y - k * 4.837512969970703125e-4
    y = y - k * 7.54978995489188216e-8
    q = k.astype(jnp.int32)
    y2 = y * y
    s = y + y * y2 * (-1.6666654611e-1 + y2 * (8.3321608736e-3 + y2 * -1.9515295891e-4))
    c = (1.0 - 0.5 * y2) + y2 * y2 * (
        4.166664568298827e-2 + y2 * (-1.388731625493765e-3 + y2 * 2.443315711809948e-5)
    )
    odd = (q & 1) == 1
    sn = jnp.where(odd, c, s)
    cs = jnp.where(odd, s, c)
    sn = jnp.where((q & 2) == 2, -sn, sn)
    cs = jnp.where(((q + 1) & 2) == 2, -cs, cs)
    return sn, cs


def place(col, shift, blocks):
    start = col + shift
    start = jnp.where(start < 0, start + blocks * COLS, start)
    first = jnp.right_shift(start, 7)
    offset = start & (COLS - 1)
    second = jnp.where(first == blocks - 1, 0, first + 1)
    return first, second, offset


def lanes(rows):
    return lax.broadcasted_iota(jnp.int32, (rows, COLS), 1)


def read_strip(g_ref, chan, col, shifts_ref, angle, blocks):
    total = None
    lane = lanes(TH)
    for z in range(LAYERS):
        first, second, offset = place(col, shifts_ref[angle, z], blocks)
        rows = pl.ds(chan * CHAN_ROWS, CHAN_ROWS)
        part0 = g_ref[first, rows, :].astype(F32)[z * TH : (z + 1) * TH]
        part1 = g_ref[second, rows, :].astype(F32)[z * TH : (z + 1) * TH]
        both = jnp.where(lane >= offset, part0, part1)
        strip = pltpu.roll(both, (COLS - offset) & (COLS - 1), 1)
        total = strip if total is None else total + strip
    return total


def halo_kernel(blocks, g_ref, shifts_ref, prev_ref, out_ref):
    angle = lax.axis_index("ang")
    col = jnp.clip(prev_ref[0, 1], 0, blocks * COLS - PIX)
    for chan in range(2):
        out_ref[chan] = read_strip(g_ref, chan, col, shifts_ref, angle, blocks)[:PIX]


def slot_row(pos_ref, slot):
    return jnp.clip(pos_ref[0, slot, 0], 0, TH if slot == 0 else TH - PIX)


def slot_col(pos_ref, slot, blocks):
    return jnp.clip(pos_ref[0, slot, 1], 0, blocks * COLS - PIX)


def scan_kernel(
    blocks,
    g_ref,
    halo_ref,
    field_ref,
    amp_ref,
    m1h_ref,
    m1l_ref,
    m2h_ref,
    m2l_ref,
    shifts_ref,
    pos_ref,
    count_ref,
    grad_ref,
    down_ref,
    strip_ref,
    trans_ref,
    back_ref,
):
    angle = lax.axis_index("ang")
    probe_re = field_ref[0]
    probe_im = field_ref[1]
    exit_re, exit_im = [], []
    for slot in range(SLOTS):
        col = slot_col(pos_ref, slot, blocks)
        row = slot_row(pos_ref, slot)
        for chan in range(2):
            strip_ref[slot, chan, :TH] = read_strip(g_ref, chan, col, shifts_ref, angle, blocks)
            if slot == 0:
                strip_ref[slot, chan, TH:] = halo_ref[chan]
        phase = strip_ref[slot, 0, pl.ds(row, PIX), :]
        damping = jnp.exp(-strip_ref[slot, 1, pl.ds(row, PIX), :])
        sn, cs = sin_cos(phase)
        tre = damping * cs
        tim = damping * sn
        trans_ref[slot, 0] = tre
        trans_ref[slot, 1] = tim
        exit_re.append(probe_re * tre - probe_im * tim)
        exit_im.append(probe_re * tim + probe_im * tre)
    data = jnp.concatenate(
        [jnp.concatenate(exit_re, axis=1), jnp.concatenate(exit_im, axis=1)], axis=0
    )
    left = left_product(m1h_ref[...], m1l_ref[...], data)
    wide = jnp.concatenate(
        [
            jnp.concatenate(
                [left[:PIX, j * PIX : (j + 1) * PIX], left[PIX:, j * PIX : (j + 1) * PIX]], axis=1
            )
            for j in range(SLOTS)
        ],
        axis=0,
    )
    far = right_product(wide, m2h_ref[...], m2l_ref[...])
    residual = []
    for slot in range(SLOTS):
        rows = far[slot * PIX : (slot + 1) * PIX]
        re, im = rows[:, :PIX], rows[:, PIX:]
        live = (slot < count_ref[0, 0]).astype(F32)
        inverse = lax.rsqrt(jnp.maximum(re * re + im * im, AMP_FLOOR * AMP_FLOOR))
        factor = (1.0 - amp_ref[0, slot] * inverse) * live
        residual.append(jnp.concatenate([re * factor, im * factor], axis=1))
    back = right_product(jnp.concatenate(residual, axis=0), m1h_ref[...], m1l_ref[...])
    tall = jnp.concatenate(
        [
            jnp.concatenate([back[j * PIX : (j + 1) * PIX, :PIX] for j in range(SLOTS)], axis=1),
            jnp.concatenate([back[j * PIX : (j + 1) * PIX, PIX:] for j in range(SLOTS)], axis=1),
        ],
        axis=0,
    )
    grad = left_product(m2h_ref[...], m2l_ref[...], tall)
    for slot in range(SLOTS):
        bre = grad[:PIX, slot * PIX : (slot + 1) * PIX]
        bim = grad[PIX:, slot * PIX : (slot + 1) * PIX]
        gre = probe_re * bre + probe_im * bim
        gim = probe_re * bim - probe_im * bre
        tre = trans_ref[slot, 0]
        tim = trans_ref[slot, 1]
        row = slot_row(pos_ref, slot)
        total_rows = TH + PIX if slot == 0 else TH
        for chan, value in enumerate((tre * gim - tim * gre, -(tre * gre + tim * gim))):
            back_ref[chan, :total_rows] = jnp.zeros((total_rows, PIX), F32)
            back_ref[chan, pl.ds(row, PIX), :] = value
            grad_ref[slot, chan] = back_ref[chan, :TH]
            if slot == 0:
                down_ref[chan] = back_ref[chan, TH:]


def spread_kernel(blocks, grad_ref, up_ref, shifts_ref, pos_ref, prev_ref, out_ref, acc_ref):
    angle = lax.axis_index("ang")
    acc_ref[...] = jnp.zeros_like(acc_ref)
    lane = lanes(TH)
    for slot in range(SLOTS + 1):
        if slot < SLOTS:
            col = slot_col(pos_ref, slot, blocks)
        else:
            col = jnp.clip(prev_ref[0, 1], 0, blocks * COLS - PIX)
        for chan in range(2):
            if slot < SLOTS:
                value = grad_ref[slot, chan]
            else:
                value = jnp.concatenate([up_ref[chan], jnp.zeros((TH - PIX, PIX), F32)], axis=0)
            for z in range(LAYERS):
                first, second, offset = place(col, shifts_ref[angle, z], blocks)
                rolled = pltpu.roll(value, offset, 1)
                rows = pl.ds(chan * CHAN_ROWS + z * TH, TH)
                acc_ref[first, rows, :] += jnp.where(lane >= offset, rolled, 0.0)
                acc_ref[second, rows, :] += jnp.where(lane < offset, rolled, 0.0)
    for b in range(blocks):
        out_ref[b] = acc_ref[b].astype(BF16)


VMEM = pl.BlockSpec(memory_space=pltpu.VMEM)
SMEM = pl.BlockSpec(memory_space=pltpu.SMEM)
PARAMS = pltpu.CompilerParams(vmem_limit_bytes=48 << 20)


def shift_rows(value, steps):
    count = lax.axis_size("rows")
    first, last = max(0, -steps), min(count, count - steps)
    return lax.ppermute(value, "rows", [(i, i + steps) for i in range(first, last)])


def on_device(delta_obj, beta_obj, layer_shifts, field, amplitudes, positions, counts):
    blocks = lax.axis_size("ang")
    m1h, m1l, m2h, m2l = dft_constants()
    prev = shift_rows(positions[0, :1], 1)
    own = jnp.concatenate(
        [obj[:, z, :].astype(BF16) for obj in (delta_obj, beta_obj) for z in range(LAYERS)], axis=0
    )
    gathered = lax.all_gather(own, "ang")
    strip = pl.pallas_call(
        functools.partial(halo_kernel, blocks),
        out_shape=jax.ShapeDtypeStruct((2, PIX, PIX), F32),
        in_specs=[VMEM, SMEM, SMEM],
        out_specs=VMEM,
        compiler_params=PARAMS,
    )(gathered, layer_shifts, prev)
    halo = shift_rows(strip, -1)
    grads, down = pl.pallas_call(
        functools.partial(scan_kernel, blocks),
        out_shape=(
            jax.ShapeDtypeStruct((SLOTS, 2, TH, PIX), F32),
            jax.ShapeDtypeStruct((2, PIX, PIX), F32),
        ),
        in_specs=[VMEM] * 8 + [SMEM] * 3,
        out_specs=(VMEM, VMEM),
        scratch_shapes=[
            pltpu.VMEM((SLOTS, 2, TH + PIX, PIX), F32),
            pltpu.VMEM((SLOTS, 2, PIX, PIX), F32),
            pltpu.VMEM((2, TH + PIX, PIX), F32),
        ],
        compiler_params=PARAMS,
    )(gathered, halo, field, amplitudes, m1h, m1l, m2h, m2l, layer_shifts, positions, counts)
    up = shift_rows(down, 1)
    spread = pl.pallas_call(
        functools.partial(spread_kernel, blocks),
        out_shape=jax.ShapeDtypeStruct((blocks, BLOCK_ROWS, COLS), BF16),
        in_specs=[VMEM, VMEM, SMEM, SMEM, SMEM],
        out_specs=VMEM,
        scratch_shapes=[pltpu.VMEM((blocks, BLOCK_ROWS, COLS), F32)],
        compiler_params=PARAMS,
    )(grads, up, layer_shifts, positions, prev)
    total = lax.psum_scatter(spread, "ang", scatter_dimension=0)
    total = total.astype(F32).reshape(2, LAYERS, TH, COLS)
    total = jnp.transpose(total, (0, 2, 1, 3))
    return (total[0], total[1])


def solution(mesh):
    placed = (
        P("rows", None, "ang"),
        P("rows", None, "ang"),
        P(),
        P(),
        P("ang", "rows", None, None),
        P("ang", "rows", None),
        P("ang", "rows"),
    )
    return jax.shard_map(
        on_device,
        mesh=mesh,
        in_specs=placed,
        out_specs=(P("rows", None, "ang"), P("rows", None, "ang")),
        check_vma=False,
    )
```

profile of v0, /device:TPU:6, one launch (start us, length us, event | category | flops | bytes accessed | tf_op | source)
XLA Modules:
  0.0 164.3 jit_solution(14805050864588333522)
XLA Ops:
  7.2 0.0 copy-start.4
  7.2 0.0 copy-start.5
  7.2 0.0 copy-start.6
  7.2 0.0 copy-start.7
  7.2 0.0 copy-start.8
  7.2 0.0 copy-start.2
  7.2 0.0 copy-start.3
  7.2 0.0 all-gather.3.cloned.1.call-start
  7.3 1.1 copy.33
  8.4 0.9 copy.32
  9.3 0.7 pad_maximum_fusion
  10.0 0.0 all-gather.3.cloned.1.call-update
  10.0 0.0 reduce-scatter.2.cloned.1.call-start
  10.1 0.8 slice_reduce_fusion
  10.9 1.9 %collective-permute-start = (s32[1,2]{1,0:T(1,128)S(1)}, s32[1,2]{1,0:T(1,128)S(1)}, u32[]{:S(2)}, u32[]{:S(2)}) collective-permute-start(s32[1,2]{1,0:T(1,128)S(1)} %bitcast.23), channel_id=1, source_target_pairs={{0,12},{12,24},{24,36},{36,48},{48,60},{60,72},{72,84},{84,96},{96... | collective-permute-start | bytes 32 | tf_op jit(solution)/shard_map/ppermute | solution.py:242
  12.8 0.8 copy.23.shifts_ref
  13.6 4.3 %collective-permute-done.prev_ref = s32[1,2]{1,0:T(1,128)S(1)} collective-permute-done((s32[1,2]{1,0:T(1,128)S(1)}, s32[1,2]{1,0:T(1,128)S(1)}, u32[]{:S(2)}, u32[]{:S(2)}) %collective-permute-start) | collective-permute-done | bytes 40 | tf_op jit(solution)/shard_map/ppermute | solution.py:242
  17.8 60.7 %all-gather.3.cloned.1.call-done = bf16[6528,128]{1,0:T(8,128)(2,1)} async-done(((bf16[544,128]{1,0:T(8,128)(2,1)}), bf16[6528,128]{1,0:T(8,128)(2,1)}) %all-gather.3.cloned.1.call-update) | async-done | bytes 1671184 | tf_op jit(solution)/shard_map/all_gather | solution.py:252
  78.5 1.4 copy-done
  80.0 0.8 shard_map.122
  80.8 1.9 %collective-permute-start.1 = (f32[2,128,128]{2,1,0:T(8,128)S(1)}, f32[2,128,128]{2,1,0:T(8,128)S(1)}, u32[]{:S(2)}, u32[]{:S(2)}) collective-permute-start(f32[2,128,128]{2,1,0:T(8,128)S(1)} %shard_map.122), channel_id=1, source_target_pairs={{12,0},{24,12},{36,24},{48,36},{60,48},{72,60},{84,72},{96,84},{10... | collective-permute-start | bytes 393224 | tf_op jit(solution)/shard_map/ppermute | solution.py:242
  82.7 0.1 copy.25.pos_ref
  83.4 1.7 %collective-permute-done.1.halo_ref = f32[2,128,128]{2,1,0:T(8,128)S(1)} collective-permute-done((f32[2,128,128]{2,1,0:T(8,128)S(1)}, f32[2,128,128]{2,1,0:T(8,128)S(1)}, u32[]{:S(2)}, u32[]{:S(2)}) %collective-permute-start.1) | collective-permute-done | bytes 131104 | tf_op jit(solution)/shard_map/ppermute | solution.py:242
  85.2 0.0 copy-done.6
  85.2 3.0 %shard_map.123 = (f32[4,2,136,128]{3,2,1,0:T(8,128)S(1)}, f32[2,128,128]{2,1,0:T(8,128)S(1)}) custom-call(bf16[12,544,128]{2,1,0:T(8,128)(2,1)S(1)} %bitcast.20, f32[2,128,128]{2,1,0:T(8,128)S(1)} %collective-permute-done.1.halo_ref, f32[2,128,128]{2,1,0:T(8,128)S(1)} %copy-done.3, f32[1,4,128,128]{3,2,1,0:T(8,128)S(1)} %copy-done.2, ...), custom_call_target="tpu_custom_call" | custom-call | tf_op jit(solution)/shard_map/pallas_call | solution.py:261
  88.2 3.6 %collective-permute-start.2 = (f32[2,128,128]{2,1,0:T(8,128)S(1)}, f32[2,128,128]{2,1,0:T(8,128)S(1)}, u32[]{:S(2)}, u32[]{:S(2)}) collective-permute-start(f32[2,128,128]{2,1,0:T(8,128)S(1)} %get-tuple-element.5), channel_id=1, source_target_pairs={{0,12},{12,24},{24,36},{36,48},{48,60},{60,72},{72,84},{84,96},{96... | collective-permute-start | bytes 393224 | tf_op jit(solution)/shard_map/ppermute | solution.py:242
  91.9 4.9 %collective-permute-done.2.up_ref = f32[2,128,128]{2,1,0:T(8,128)S(1)} collective-permute-done((f32[2,128,128]{2,1,0:T(8,128)S(1)}, f32[2,128,128]{2,1,0:T(8,128)S(1)}, u32[]{:S(2)}, u32[]{:S(2)}) %collective-permute-start.2) | collective-permute-done | bytes 131104 | tf_op jit(solution)/shard_map/ppermute | solution.py:242
  96.8 2.7 %shard_map.124 = bf16[12,544,128]{2,1,0:T(8,128)(2,1)} custom-call(f32[4,2,136,128]{3,2,1,0:T(8,128)S(1)} %get-tuple-element.4.grad_ref, f32[2,128,128]{2,1,0:T(8,128)S(1)} %collective-permute-done.2.up_ref, s32[12,2]{1,0:T(8,128)S(1)} %copy.23.shifts_ref, s32[1,4,2]{2,1,0:T(4,128)S(1)} %copy.25.pos_ref, s32[1,2]{1,0:T(1,128)S(1)} %collective-permute-done.prev_ref), custom_call_target="tpu_custom_call" | custom-call | tf_op jit(solution)/shard_map/pallas_call | solution.py:277
  99.4 0.0 reduce-scatter.2.cloned.1.call-update
  99.5 56.2 %reduce-scatter.2.cloned.1.call-done = bf16[1,544,128]{2,1,0:T(8,128)(2,1)} async-done(((bf16[12,544,128]{2,1,0:T(8,128)(2,1)}), bf16[1,544,128]{2,1,0:T(8,128)(2,1)}) %reduce-scatter.2.cloned.1.call-update) | async-done | bytes 139280 | tf_op jit(solution)/shard_map/reduce_scatter | solution.py:285
  155.7 1.0 copy.34
  156.7 0.7 slice_bitcast_fusion
  (10 shorter events, 0.0 us)
Async XLA Ops:
  7.2 78.0 %copy-start.4 = (bf16[256,256]{1,0:T(8,128)(2,1)S(1)}, bf16[256,256]{1,0:T(8,128)(2,1)}, u32[]{:S(2)}) copy-start(bf16[256,256]{1,0:T(8,128)(2,1)} %constant.11.clone.m2l_ref) | copy-start | bytes 393220
  7.2 78.0 %copy-start.5 = (bf16[256,256]{1,0:T(8,128)(2,1)S(1)}, bf16[256,256]{1,0:T(8,128)(2,1)}, u32[]{:S(2)}) copy-start(bf16[256,256]{1,0:T(8,128)(2,1)} %constant.10.clone.m2h_ref) | copy-start | bytes 393220
  7.2 78.0 %copy-start.6 = (bf16[256,256]{1,0:T(8,128)(2,1)S(1)}, bf16[256,256]{1,0:T(8,128)(2,1)}, u32[]{:S(2)}) copy-start(bf16[256,256]{1,0:T(8,128)(2,1)} %constant.9.clone.m1l_ref) | copy-start | bytes 393220
  7.2 78.0 %copy-start.7 = (bf16[256,256]{1,0:T(8,128)(2,1)S(1)}, bf16[256,256]{1,0:T(8,128)(2,1)}, u32[]{:S(2)}) copy-start(bf16[256,256]{1,0:T(8,128)(2,1)} %constant.8.clone.m1h_ref) | copy-start | bytes 393220
  7.2 75.5 %copy-start.8 = (s32[1,4,2]{1,2,0:T(2,128)S(1)}, s32[1,4,2]{1,2,0:T(2,128)}, u32[]{:S(2)}) copy-start(s32[1,4,2]{1,2,0:T(2,128)} %param.16) | copy-start | bytes 100
  7.2 78.0 %copy-start.2 = (f32[1,4,128,128]{3,2,1,0:T(8,128)S(1)}, f32[1,4,128,128]{3,2,1,0:T(8,128)}, u32[]{:S(2)}) copy-start(f32[1,4,128,128]{3,2,1,0:T(8,128)} %amp_ref.1) | copy-start | bytes 786436
  7.2 78.0 %copy-start.3 = (f32[2,128,128]{2,1,0:T(8,128)S(1)}, f32[2,128,128]{2,1,0:T(8,128)}, u32[]{:S(2)}) copy-start(f32[2,128,128]{2,1,0:T(8,128)} %field_ref.1) | copy-start | bytes 393220
  7.2 71.3 %all-gather.3.cloned.1.call-start = ((), (), s32[]{:S(2)}) async-start(), calls=%async_computation.2 | async-start | bytes 1810432 | tf_op jit(solution)/shard_map/all_gather | solution.py:252
  10.0 145.7 %reduce-scatter.2.cloned.1.call-start = ((), (), s32[]{:S(2)}) async-start(), calls=%async_computation.1 | async-start | bytes 1810432 | tf_op jit(solution)/shard_map/reduce_scatter | solution.py:285
  10.9 7.0 %collective-permute-start = (s32[1,2]{1,0:T(1,128)S(1)}, s32[1,2]{1,0:T(1,128)S(1)}, u32[]{:S(2)}, u32[]{:S(2)}) collective-permute-start(s32[1,2]{1,0:T(1,128)S(1)} %bitcast.23), channel_id=1, source_target_pairs={{0,12},{12,24},{24,36},{36,48},{48,60},{60,72},{72,84},{84,96},{96... | collective-permute-start | bytes 32 | tf_op jit(solution)/shard_map/ppermute | solution.py:242
  78.5 1.4 copy-start
  79.9 5.3 %copy-start.1 = (bf16[6528,128]{1,0:T(8,128)(2,1)S(1)}, bf16[6528,128]{1,0:T(8,128)(2,1)}, u32[]{:S(2)}) copy-start(bf16[6528,128]{1,0:T(8,128)(2,1)} %all-gather.3.cloned.1.call-done) | copy-start | bytes 5013508
  80.8 4.4 %collective-permute-start.1 = (f32[2,128,128]{2,1,0:T(8,128)S(1)}, f32[2,128,128]{2,1,0:T(8,128)S(1)}, u32[]{:S(2)}, u32[]{:S(2)}) collective-permute-start(f32[2,128,128]{2,1,0:T(8,128)S(1)} %shard_map.122), channel_id=1, source_target_pairs={{12,0},{24,12},{36,24},{48,36},{60,48},{72,60},{84,72},{96,84},{10... | collective-permute-start | bytes 393224 | tf_op jit(solution)/shard_map/ppermute | solution.py:242
  88.2 8.5 %collective-permute-start.2 = (f32[2,128,128]{2,1,0:T(8,128)S(1)}, f32[2,128,128]{2,1,0:T(8,128)S(1)}, u32[]{:S(2)}, u32[]{:S(2)}) collective-permute-start(f32[2,128,128]{2,1,0:T(8,128)S(1)} %get-tuple-element.5), channel_id=1, source_target_pairs={{0,12},{12,24},{24,36},{36,48},{48,60},{60,72},{72,84},{84,96},{96... | collective-permute-start | bytes 393224 | tf_op jit(solution)/shard_map/ppermute | solution.py:242
Sparse Core Ops, SparseCore 0:
  11.0 67.4 all-gather.2
  99.6 56.0 reduce-scatter.1
where the time goes:
time: 165 us; the launch traced here: 164 us
  waiting for transfers between devices  128 us (78%)
  between operations  14.8 us (9%)
  starting transfers between devices  7.55 us (5%)
  local copies, waits for them, and re-layouts  6.91 us (4%)
  Pallas kernels  6.46 us (4%)
    all_gather x1, waiting for transfers between devices, on_device(): gathered = lax.all_gather(own, 'ang')  60.7 us
    reduce_scatter x1, waiting for transfers between devices, on_device(): total = lax.psum_scatter(spread, 'ang', scatter_dimension=0)  56.2 us
    ppermute x3, waiting for transfers between devices, shift_rows(): lax.ppermute(value, 'rows', [(i, i + steps) for i in range(first, last)])  10.9 us
    ppermute x3, starting transfers between devices, shift_rows(): lax.ppermute(value, 'rows', [(i, i + steps) for i in range(first, last)])  7.48 us
    unnamed x22, local copies, waits for them, and re-layouts  4.36 us
  transfers between devices with their start and end apart: 5, of which 5 were waited for; matrix products, arithmetic and copies ran while one was open for 1% of the time, Pallas kernels for 0%

commit v1 on v0

--- a/solution.py
+++ b/solution.py
@@ -231,9 +231,165 @@
         out_ref[b] = acc_ref[b].astype(BF16)
 
 
+CHUNKS = ((0, 144), (144, 128), (272, 144), (416, 128))
+FIRST_HALF = (0, 1)
+SECOND_HALF = (2, 3)
+ALL_CHUNKS = (0, 1, 2, 3)
+
+
+def ring(blocks):
+    me = lax.axis_index("ang")
+    right = lax.rem(me + 1, blocks)
+    left = lax.rem(me + blocks - 1, blocks)
+    return me, right, left
+
+
+def greet(neighbours):
+    barrier = pltpu.get_barrier_semaphore()
+    for neighbour in neighbours:
+        pl.semaphore_signal(barrier, inc=1, device_id={"ang": neighbour})
+    pl.semaphore_wait(barrier, len(neighbours))
+
+
+def send(src, dst, send_sem, recv_sem, target):
+    return pltpu.make_async_remote_copy(
+        src_ref=src, dst_ref=dst, send_sem=send_sem, recv_sem=recv_sem, device_id={"ang": target}
+    )
+
+
+def gather_kernel(blocks, delta_ref, beta_ref, out_ref, send_r, recv_r, send_l, recv_l):
+    me, right, left = ring(blocks)
+    half = blocks // 2
+    for chan, ref in enumerate((delta_ref, beta_ref)):
+        layers = [ref[pl.ds(z, TH, stride=LAYERS), :] for z in range(LAYERS)]
+        rows = pl.ds(chan * CHAN_ROWS, CHAN_ROWS)
+        out_ref[me, rows, :] = jnp.concatenate(layers, axis=0).astype(BF16)
+    greet((left, right))
+
+    def copy(step, chunk, to_right):
+        origin = lax.rem(me - step + blocks, blocks) if to_right else lax.rem(me + step, blocks)
+        part = out_ref.at[origin, pl.ds(*CHUNKS[chunk]), :]
+        if to_right:
+            return send(part, part, send_r.at[step, chunk], recv_r.at[step, chunk], right)
+        return send(part, part, send_l.at[step, chunk], recv_l.at[step, chunk], left)
+
+    def arrival(step, chunk, from_left):
+        origin = lax.rem(me - step - 1 + blocks, blocks) if from_left else lax.rem(me + step + 1, blocks)
+        part = out_ref.at[origin, pl.ds(*CHUNKS[chunk]), :]
+        if from_left:
+            return send(part, part, send_r.at[step, chunk], recv_r.at[step, chunk], right)
+        return send(part, part, send_l.at[step, chunk], recv_l.at[step, chunk], left)
+
+    def carried(step, to_right):
+        if step < half - 1:
+            return ALL_CHUNKS
+        return FIRST_HALF if to_right else SECOND_HALF
+
+    started = []
+    for step in range(half):
+        for chunk in ALL_CHUNKS:
+            for to_right in (True, False):
+                if step > 0:
+                    arrival(step - 1, chunk, to_right).wait_recv()
+                if chunk in carried(step, to_right):
+                    item = copy(step, chunk, to_right)
+                    item.start()
+                    started.append(item)
+    for to_right in (True, False):
+        for chunk in carried(half - 1, to_right):
+            arrival(half - 1, chunk, to_right).wait_recv()
+    for item in started:
+        item.wait_send()
+
+
+def reduce_kernel(
+    blocks,
+    spread_ref,
+    delta_ref,
+    beta_ref,
+    out_r,
+    out_l,
+    in_r,
+    in_l,
+    send_r,
+    recv_r,
+    send_l,
+    recv_l,
+):
+    me, right, left = ring(blocks)
+    half = blocks // 2
+    greet((left, right))
+
+    def copy(step, chunk, to_right):
+        rows = pl.ds(*CHUNKS[chunk])
+        if to_right:
+            if step == 0:
+                src = spread_ref.at[lax.rem(me + half, blocks), rows, :]
+            else:
+                src = out_r.at[step, rows, :]
+            return send(
+                src, in_r.at[step, rows, :], send_r.at[step, chunk], recv_r.at[step, chunk], right
+            )
+        if step == 0:
+            src = spread_ref.at[lax.rem(me + half, blocks), rows, :]
+        else:
+            src = out_l.at[step, rows, :]
+        return send(
+            src, in_l.at[step, rows, :], send_l.at[step, chunk], recv_l.at[step, chunk], left
+        )
+
+    def carried(step, to_right):
+        if step > 0:
+            return ALL_CHUNKS
+        return FIRST_HALF if to_right else SECOND_HALF
+
+    def partial(step, chunk, to_right):
+        rows = pl.ds(*CHUNKS[chunk])
+        if to_right:
+            target = lax.rem(me + half - step, blocks)
+        else:
+            target = lax.rem(me - half + step + blocks, blocks)
+        value = spread_ref[target, rows, :]
+        if chunk in carried(step - 1, to_right):
+            copy(step - 1, chunk, to_right).wait_recv()
+            coming = in_r if to_right else in_l
+            value = (value.astype(F32) + coming[step - 1, rows, :].astype(F32)).astype(BF16)
+        going = out_r if to_right else out_l
+        going[step, rows, :] = value
+
+    started = []
+    for step in range(half):
+        for chunk in ALL_CHUNKS:
+            ways = [way for way in (True, False) if chunk in carried(step, way)]
+            if step > 0:
+                for way in ways:
+                    partial(step, chunk, way)
+            for way in ways:
+                item = copy(step, chunk, way)
+                item.start()
+                started.append(item)
+    for chunk in ALL_CHUNKS:
+        for way in (True, False):
+            copy(half - 1, chunk, way).wait_recv()
+    for chan, ref in enumerate((delta_ref, beta_ref)):
+        rows = pl.ds(chan * CHAN_ROWS, CHAN_ROWS)
+        total = in_r[half - 1, rows, :].astype(F32) + in_l[half - 1, rows, :].astype(F32)
+        total = total + spread_ref[me, rows, :].astype(F32)
+        for z in range(LAYERS):
+            ref[pl.ds(z, TH, stride=LAYERS), :] = total[z * TH : (z + 1) * TH]
+    for item in started:
+        item.wait_send()
+
+
 VMEM = pl.BlockSpec(memory_space=pltpu.VMEM)
 SMEM = pl.BlockSpec(memory_space=pltpu.SMEM)
 PARAMS = pltpu.CompilerParams(vmem_limit_bytes=48 << 20)
+
+
+def comm_params(number):
+    return pltpu.CompilerParams(
+        vmem_limit_bytes=48 << 20, collective_id=number, has_side_effects=True
+    )
 
 
 def shift_rows(value, steps):
@@ -246,10 +402,15 @@
     blocks = lax.axis_size("ang")
     m1h, m1l, m2h, m2l = dft_constants()
     prev = shift_rows(positions[0, :1], 1)
-    own = jnp.concatenate(
-        [obj[:, z, :].astype(BF16) for obj in (delta_obj, beta_obj) for z in range(LAYERS)], axis=0
-    )
-    gathered = lax.all_gather(own, "ang")
+    half = blocks // 2
+    gathered = pl.pallas_call(
+        functools.partial(gather_kernel, blocks),
+        out_shape=jax.ShapeDtypeStruct((blocks, BLOCK_ROWS, COLS), BF16),
+        in_specs=[VMEM, VMEM],
+        out_specs=VMEM,
+        scratch_shapes=[pltpu.SemaphoreType.DMA((half, len(CHUNKS)))] * 4,
+        compiler_params=comm_params(0),
+    )(delta_obj.reshape(CHAN_ROWS, COLS), beta_obj.reshape(CHAN_ROWS, COLS))
     strip = pl.pallas_call(
         functools.partial(halo_kernel, blocks),
         out_shape=jax.ShapeDtypeStruct((2, PIX, PIX), F32),
@@ -282,10 +443,18 @@
         scratch_shapes=[pltpu.VMEM((blocks, BLOCK_ROWS, COLS), F32)],
         compiler_params=PARAMS,
     )(grads, up, layer_shifts, positions, prev)
-    total = lax.psum_scatter(spread, "ang", scatter_dimension=0)
-    total = total.astype(F32).reshape(2, LAYERS, TH, COLS)
-    total = jnp.transpose(total, (0, 2, 1, 3))
-    return (total[0], total[1])
+    grad = jax.ShapeDtypeStruct((CHAN_ROWS, COLS), F32)
+    delta_grad, beta_grad = pl.pallas_call(
+        functools.partial(reduce_kernel, blocks),
+        out_shape=(grad, grad),
+        in_specs=[VMEM],
+        out_specs=(VMEM, VMEM),
+        scratch_shapes=[pltpu.VMEM((half, BLOCK_ROWS, COLS), BF16)] * 4
+        + [pltpu.SemaphoreType.DMA((half, len(CHUNKS)))] * 4,
+        compiler_params=comm_params(1),
+    )(spread)
+    shape = (TH, LAYERS, COLS)
+    return (delta_grad.reshape(shape), beta_grad.reshape(shape))
 
 
 def solution(mesh):

time: 165 us -> 89.8 us (0.54)
  waiting for transfers between devices: 128 us -> 7.01 us
  Pallas kernels: 6.46 us -> 68.2 us
  between operations: 14.8 us -> 1.41 us
  local copies, waits for them, and re-layouts: 6.91 us -> 4.82 us
    pallas_call x0 -> x2, Pallas kernels: none -> 63 us  [the longest x1 36 us: on_device(): pl.pallas_call(functools.partial(gather_kernel, blocks), out_shape=jax.Sh...]
    all_gather x1 -> x0, waiting for transfers between devices: 60.7 us -> none  [on_device(): gathered = lax.all_gather(own, 'ang')]
    reduce_scatter x1 -> x0, waiting for transfers between devices: 56.2 us -> none  [on_device(): total = lax.psum_scatter(spread, 'ang', scatter_dimension=0)]
    ppermute x3, waiting for transfers between devices: 10.9 us -> 7.01 us  [shift_rows(): lax.ppermute(value, 'rows', [(i, i + steps) for i in range(first, last)])]
  transfers between devices with their start and end apart: 5 -> 3, of which waited for: 5 -> 2; matrix products, arithmetic and copies ran while one was open for 1% -> 1% of each run, Pallas kernels for 0% -> 40%
where the time goes in v1:
time: 89.8 us; the launch traced here: 89 us
  Pallas kernels  68.2 us (76%)
  starting transfers between devices  7.57 us (8%)
  waiting for transfers between devices  7.01 us (8%)
  local copies, waits for them, and re-layouts  4.82 us (5%)
  between operations  1.41 us (2%)
    pallas_call x1, Pallas kernels, on_device(): pl.pallas_call(functools.partial(gather_kernel, blocks), out_shape=jax.Sh...  36 us
    pallas_call x1, Pallas kernels, on_device(): pl.pallas_call(functools.partial(reduce_kernel, blocks), out_shape=(grad,...  26.9 us
    ppermute x3, starting transfers between devices, shift_rows(): lax.ppermute(value, 'rows', [(i, i + steps) for i in range(first, last)])  7.57 us
    ppermute x3, waiting for transfers between devices, shift_rows(): lax.ppermute(value, 'rows', [(i, i + steps) for i in range(first, last)])  7.01 us
    unnamed x22, local copies, waits for them, and re-layouts  4.03 us
    pallas_call x1, Pallas kernels, on_device(): pl.pallas_call(functools.partial(scan_kernel, blocks), out_shape=(jax.Sha...  3.01 us
  transfers between devices with their start and end apart: 3, of which 2 were waited for; matrix products, arithmetic and copies ran while one was open for 1% of the time, Pallas kernels for 40%

profile of v1, /device:TPU:6, one launch (start us, length us, event | category | flops | bytes accessed | tf_op | source)
XLA Modules:
  0.0 89.0 jit_solution(13058646226158485713)
XLA Ops:
  0.6 0.8 slice_reduce_fusion
  1.4 1.9 %collective-permute-start = (s32[1,2]{1,0:T(1,128)S(1)}, s32[1,2]{1,0:T(1,128)S(1)}, u32[]{:S(2)}, u32[]{:S(2)}) collective-permute-start(s32[1,2]{1,0:T(1,128)S(1)} %bitcast.9), channel_id=1, source_target_pairs={{0,12},{12,24},{24,36},{36,48},{48,60},{60,72},{72,84},{84,96},{96... | collective-permute-start | bytes 32 | tf_op jit(solution)/shard_map/ppermute | solution.py:398
  3.3 0.8 copy.13.shifts_ref
  4.1 0.0 copy-start.1
  4.1 0.9 %copy-done.1 = f32[136,2,128]{2,1,0:T(2,128)S(1)} copy-done((f32[136,2,128]{2,1,0:T(2,128)S(1)}, f32[136,2,128]{2,1,0:T(2,128)}, u32[]{:S(2)}) %copy-start.1) | copy-done | bytes 139288
  5.0 0.0 copy-start.2
  5.0 0.9 %copy-done.2 = f32[136,2,128]{2,1,0:T(2,128)S(1)} copy-done((f32[136,2,128]{2,1,0:T(2,128)S(1)}, f32[136,2,128]{2,1,0:T(2,128)}, u32[]{:S(2)}) %copy-start.2) | copy-done | bytes 139288
  5.9 0.0 copy-start.8
  5.9 0.0 copy-start
  5.9 0.0 copy-start.5
  6.0 0.0 copy-start.6
  6.0 0.0 copy-start.7
  6.0 36.0 %shard_map.122.g_ref = bf16[12,544,128]{2,1,0:T(8,128)(2,1)S(1)} custom-call(f32[272,128]{1,0:T(8,128)S(1)} %bitcast.7, f32[272,128]{1,0:T(8,128)S(1)} %bitcast.8), custom_call_target="tpu_custom_call" | custom-call | tf_op jit(solution)/shard_map/pallas_call | solution.py:406
  42.0 0.0 collective-permute-done.prev_ref
  42.0 0.8 shard_map.123
  42.8 2.4 %collective-permute-start.1 = (f32[2,128,128]{2,1,0:T(8,128)S(1)}, f32[2,128,128]{2,1,0:T(8,128)S(1)}, u32[]{:S(2)}, u32[]{:S(2)}) collective-permute-start(f32[2,128,128]{2,1,0:T(8,128)S(1)} %shard_map.123), channel_id=1, source_target_pairs={{12,0},{24,12},{36,24},{48,36},{60,48},{72,60},{84,72},{96,84},{10... | collective-permute-start | bytes 393224 | tf_op jit(solution)/shard_map/ppermute | solution.py:398
  45.2 0.0 copy-done.8
  45.2 0.1 copy.15.pos_ref
  46.0 1.7 %collective-permute-done.1.halo_ref = f32[2,128,128]{2,1,0:T(8,128)S(1)} collective-permute-done((f32[2,128,128]{2,1,0:T(8,128)S(1)}, f32[2,128,128]{2,1,0:T(8,128)S(1)}, u32[]{:S(2)}, u32[]{:S(2)}) %collective-permute-start.1) | collective-permute-done | bytes 131104 | tf_op jit(solution)/shard_map/ppermute | solution.py:398
  47.7 0.0 copy-done
  47.7 0.0 copy-done.3
  47.7 0.0 copy-done.4
  47.7 0.0 copy-done.5
  47.7 0.0 copy-done.6
  47.7 0.0 copy-done.7
  47.7 3.0 %shard_map.124 = (f32[4,2,136,128]{3,2,1,0:T(8,128)S(1)}, f32[2,128,128]{2,1,0:T(8,128)S(1)}) custom-call(bf16[12,544,128]{2,1,0:T(8,128)(2,1)S(1)} %shard_map.122.g_ref, f32[2,128,128]{2,1,0:T(8,128)S(1)} %collective-permute-done.1.halo_ref, f32[2,128,128]{2,1,0:T(8,128)S(1)} %copy-done.3, f32[1,4,128,128]{3,2,1,0:T(8,128)S(1)} %copy-done, ...), custom_call_target="tpu_custom_call" | custom-call | tf_op jit(solution)/shard_map/pallas_call | solution.py:422
  50.8 3.3 %collective-permute-start.2 = (f32[2,128,128]{2,1,0:T(8,128)S(1)}, f32[2,128,128]{2,1,0:T(8,128)S(1)}, u32[]{:S(2)}, u32[]{:S(2)}) collective-permute-start(f32[2,128,128]{2,1,0:T(8,128)S(1)} %get-tuple-element.7), channel_id=1, source_target_pairs={{0,12},{12,24},{24,36},{36,48},{48,60},{60,72},{72,84},{84,96},{96... | collective-permute-start | bytes 393224 | tf_op jit(solution)/shard_map/ppermute | solution.py:398
  54.0 5.3 %collective-permute-done.2.up_ref = f32[2,128,128]{2,1,0:T(8,128)S(1)} collective-permute-done((f32[2,128,128]{2,1,0:T(8,128)S(1)}, f32[2,128,128]{2,1,0:T(8,128)S(1)}, u32[]{:S(2)}, u32[]{:S(2)}) %collective-permute-start.2) | collective-permute-done | bytes 131104 | tf_op jit(solution)/shard_map/ppermute | solution.py:398
  59.3 1.5 %shard_map.125.spread_ref = bf16[12,544,128]{2,1,0:T(8,128)(2,1)S(1)} custom-call(f32[4,2,136,128]{3,2,1,0:T(8,128)S(1)} %get-tuple-element.6.grad_ref, f32[2,128,128]{2,1,0:T(8,128)S(1)} %collective-permute-done.2.up_ref, s32[12,2]{1,0:T(8,128)S(1)} %copy.13.shifts_ref, s32[1,4,2]{2,1,0:T(4,128)S(1)} %copy.15.pos_ref, s32[1,2]{1,0:T(1,128)S(1)} %collective-permute-done.prev_ref), custom_call_target="tpu_custom_call" | custom-call | tf_op jit(solution)/shard_map/pallas_call | solution.py:438
  60.8 26.9 %shard_map.126 = (f32[272,128]{1,0:T(8,128)S(1)}, f32[272,128]{1,0:T(8,128)S(1)}) custom-call(bf16[12,544,128]{2,1,0:T(8,128)(2,1)S(1)} %shard_map.125.spread_ref), custom_call_target="tpu_custom_call" | custom-call | tf_op jit(solution)/shard_map/pallas_call | solution.py:447
  87.7 0.7 copy.21
  88.4 0.7 copy.22
  (2 shorter events, 0.0 us)
Async XLA Ops:
  1.4 40.6 %collective-permute-start = (s32[1,2]{1,0:T(1,128)S(1)}, s32[1,2]{1,0:T(1,128)S(1)}, u32[]{:S(2)}, u32[]{:S(2)}) collective-permute-start(s32[1,2]{1,0:T(1,128)S(1)} %bitcast.9), channel_id=1, source_target_pairs={{0,12},{12,24},{24,36},{36,48},{48,60},{60,72},{72,84},{84,96},{96... | collective-permute-start | bytes 32 | tf_op jit(solution)/shard_map/ppermute | solution.py:398
  4.1 0.9 %copy-start.1 = (f32[136,2,128]{2,1,0:T(2,128)S(1)}, f32[136,2,128]{2,1,0:T(2,128)}, u32[]{:S(2)}) copy-start(f32[136,2,128]{2,1,0:T(2,128)} %param.11) | copy-start | bytes 417796
  5.0 0.9 %copy-start.2 = (f32[136,2,128]{2,1,0:T(2,128)S(1)}, f32[136,2,128]{2,1,0:T(2,128)}, u32[]{:S(2)}) copy-start(f32[136,2,128]{2,1,0:T(2,128)} %param.12) | copy-start | bytes 417796
  5.9 39.3 %copy-start.8 = (s32[1,4,2]{1,2,0:T(2,128)S(1)}, s32[1,4,2]{1,2,0:T(2,128)}, u32[]{:S(2)}) copy-start(s32[1,4,2]{1,2,0:T(2,128)} %param.16) | copy-start | bytes 100
  5.9 41.8 %copy-start = (f32[1,4,128,128]{3,2,1,0:T(8,128)S(1)}, f32[1,4,128,128]{3,2,1,0:T(8,128)}, u32[]{:S(2)}) copy-start(f32[1,4,128,128]{3,2,1,0:T(8,128)} %amp_ref.1) | copy-start | bytes 786436
  5.9 41.8 %copy-start.3 = (f32[2,128,128]{2,1,0:T(8,128)S(1)}, f32[2,128,128]{2,1,0:T(8,128)}, u32[]{:S(2)}) copy-start(f32[2,128,128]{2,1,0:T(8,128)} %field_ref.1) | copy-start | bytes 393220
  5.9 41.8 %copy-start.4 = (bf16[256,256]{1,0:T(8,128)(2,1)S(1)}, bf16[256,256]{1,0:T(8,128)(2,1)}, u32[]{:S(2)}) copy-start(bf16[256,256]{1,0:T(8,128)(2,1)} %constant.11.clone.m2l_ref) | copy-start | bytes 393220
  5.9 41.8 %copy-start.5 = (bf16[256,256]{1,0:T(8,128)(2,1)S(1)}, bf16[256,256]{1,0:T(8,128)(2,1)}, u32[]{:S(2)}) copy-start(bf16[256,256]{1,0:T(8,128)(2,1)} %constant.10.clone.m2h_ref) | copy-start | bytes 393220
  6.0 41.8 %copy-start.6 = (bf16[256,256]{1,0:T(8,128)(2,1)S(1)}, bf16[256,256]{1,0:T(8,128)(2,1)}, u32[]{:S(2)}) copy-start(bf16[256,256]{1,0:T(8,128)(2,1)} %constant.9.clone.m1l_ref) | copy-start | bytes 393220
  6.0 41.8 %copy-start.7 = (bf16[256,256]{1,0:T(8,128)(2,1)S(1)}, bf16[256,256]{1,0:T(8,128)(2,1)}, u32[]{:S(2)}) copy-start(bf16[256,256]{1,0:T(8,128)(2,1)} %constant.8.clone.m1h_ref) | copy-start | bytes 393220
  42.8 4.9 %collective-permute-start.1 = (f32[2,128,128]{2,1,0:T(8,128)S(1)}, f32[2,128,128]{2,1,0:T(8,128)S(1)}, u32[]{:S(2)}, u32[]{:S(2)}) collective-permute-start(f32[2,128,128]{2,1,0:T(8,128)S(1)} %shard_map.123), channel_id=1, source_target_pairs={{12,0},{24,12},{36,24},{48,36},{60,48},{72,60},{84,72},{96,84},{10... | collective-permute-start | bytes 393224 | tf_op jit(solution)/shard_map/ppermute | solution.py:398
  50.8 8.5 %collective-permute-start.2 = (f32[2,128,128]{2,1,0:T(8,128)S(1)}, f32[2,128,128]{2,1,0:T(8,128)S(1)}, u32[]{:S(2)}, u32[]{:S(2)}) collective-permute-start(f32[2,128,128]{2,1,0:T(8,128)S(1)} %get-tuple-element.7), channel_id=1, source_target_pairs={{0,12},{12,24},{24,36},{36,48},{48,60},{60,72},{72,84},{84,96},{96... | collective-permute-start | bytes 393224 | tf_op jit(solution)/shard_map/ppermute | solution.py:398

commit v2 on v0

v2 whole, which is shorter than its diff:
```python
import functools
import math

import jax
import jax.numpy as jnp
import numpy as np
from jax import lax
from jax.experimental import pallas as pl
from jax.experimental.pallas import tpu as pltpu
from jax.sharding import PartitionSpec as P

PIX = 128
TH = 136
COLS = 128
LAYERS = 2
SHIFT = 8
SLOTS = 4
AMP_FLOOR = 0.1
BLOCK_ROWS = 2 * LAYERS * TH
CHAN_ROWS = LAYERS * TH
F32 = jnp.float32
BF16 = jnp.bfloat16


def dft_constants():
    counter = np.arange(PIX)
    angle = (counter[:, None] * counter[None, :] % PIX) * (2.0 * math.pi / PIX)
    scale = 1.0 / math.sqrt(PIX)
    re = np.cos(angle) * scale
    im = -np.sin(angle) * scale
    m1 = np.block([[re, -im], [im, re]])
    m2 = np.block([[re, im], [-im, re]])

    def split(m):
        hi = m.astype(BF16)
        lo = (m - hi.astype(np.float64)).astype(BF16)
        return np.asarray(hi), np.asarray(lo)

    return split(m1) + split(m2)


def split_f32(x):
    hi = x.astype(BF16)
    lo = (x - hi.astype(F32)).astype(BF16)
    return hi, lo


def dot(a, b):
    return jnp.dot(a, b, preferred_element_type=F32)


def left_product(hi, lo, data):
    d_hi, d_lo = split_f32(data)
    return dot(hi, d_hi) + (dot(hi, d_lo) + dot(lo, d_hi))


def right_product(data, hi, lo):
    d_hi, d_lo = split_f32(data)
    return dot(d_hi, hi) + (dot(d_lo, hi) + dot(d_hi, lo))


def sin_cos(x):
    k = jnp.floor(x * (2.0 / math.pi) + 0.5)
    y = x - k * 1.5703125
    y = y - k * 4.837512969970703125e-4
    y = y - k * 7.54978995489188216e-8
    q = k.astype(jnp.int32)
    y2 = y * y
    s = y + y * y2 * (-1.6666654611e-1 + y2 * (8.3321608736e-3 + y2 * -1.9515295891e-4))
    c = (1.0 - 0.5 * y2) + y2 * y2 * (
        4.166664568298827e-2 + y2 * (-1.388731625493765e-3 + y2 * 2.443315711809948e-5)
    )
    odd = (q & 1) == 1
    sn = jnp.where(odd, c, s)
    cs = jnp.where(odd, s, c)
    sn = jnp.where((q & 2) == 2, -sn, sn)
    cs = jnp.where(((q + 1) & 2) == 2, -cs, cs)
    return sn, cs


def place(col, shift, blocks):
    start = col + shift
    start = jnp.where(start < 0, start + blocks * COLS, start)
    first = jnp.right_shift(start, 7)
    offset = start & (COLS - 1)
    second = jnp.where(first == blocks - 1, 0, first + 1)
    return first, second, offset


CHUNKS = ((0, 144), (144, 128), (272, 144), (416, 128))
FIRST_HALF = (0, 1)
SECOND_HALF = (2, 3)
ALL_CHUNKS = (0, 1, 2, 3)
STRIPS = SLOTS + 1
PREV = SLOTS


def kernel(
    blocks,
    tiles,
    delta_hbm,
    beta_hbm,
    field_hbm,
    amp_hbm,
    m1h_hbm,
    m1l_hbm,
    m2h_hbm,
    m2l_hbm,
    shifts_ref,
    pos_ref,
    count_ref,
    pos_hbm,
    delta_out,
    beta_out,
    object_ref,
    field_ref,
    amp_ref,
    m1h_ref,
    m1l_ref,
    m2h_ref,
    m2l_ref,
    prev_pos_vmem,
    prev_pos,
    g_ref,
    strip_ref,
    strip_own,
    strip_prev,
    trans_ref,
    back_ref,
    rolled_ref,
    out_r,
    out_l,
    in_r,
    in_l,
    load_sem,
    edge_send,
    edge_recv,
    send_r,
    recv_r,
    send_l,
    recv_l,
    send_r2,
    recv_r2,
    send_l2,
    recv_l2,
):
    me = lax.axis_index("ang")
    right = lax.rem(me + 1, blocks)
    left = lax.rem(me + blocks - 1, blocks)
    tile = lax.axis_index("rows")
    below = lax.rem(tile + 1, tiles)
    above = lax.rem(tile + tiles - 1, tiles)
    half = blocks // 2

    loads = [
        pltpu.make_async_copy(src, dst, load_sem.at[i])
        for i, (src, dst) in enumerate(
            (
                (delta_hbm, object_ref.at[0]),
                (beta_hbm, object_ref.at[1]),
                (amp_hbm.at[0], amp_ref.at[pl.ds(0, SLOTS)]),
                (field_hbm, field_ref),
                (m1h_hbm, m1h_ref),
                (m1l_hbm, m1l_ref),
                (m2h_hbm, m2h_ref),
                (m2l_hbm, m2l_ref),
            )
        )
    ]
    for item in loads:
        item.start()
    barrier = pltpu.get_barrier_semaphore()
    for target in ({"ang": left}, {"ang": right}, {"rows": above}, {"rows": below}):
        pl.semaphore_signal(barrier, inc=1, device_id=target)
    for chan in range(2):
        loads[chan].wait()
        layers = [object_ref[chan, pl.ds(z, TH, stride=LAYERS), :] for z in range(LAYERS)]
        rows = pl.ds(chan * CHAN_ROWS, CHAN_ROWS)
        g_ref[me, rows, :] = jnp.concatenate(layers, axis=0).astype(BF16)
    pl.semaphore_wait(barrier, 4)

    def remote(src, dst, send_sem, recv_sem, target):
        return pltpu.make_async_remote_copy(
            src_ref=src, dst_ref=dst, send_sem=send_sem, recv_sem=recv_sem, device_id=target
        )

    def edge(index, src, dst, target):
        return remote(src, dst, edge_send.at[index], edge_recv.at[index], target)

    def gather_copy(step, chunk, to_right, coming=False):
        hops = step + 1 if coming else step
        if to_right:
            origin = lax.rem(me - hops + blocks, blocks)
        else:
            origin = lax.rem(me + hops, blocks)
        part = g_ref.at[origin, pl.ds(*CHUNKS[chunk]), :]
        if to_right:
            return remote(
                part, part, send_r.at[step, chunk], recv_r.at[step, chunk], {"ang": right}
            )
        return remote(part, part, send_l.at[step, chunk], recv_l.at[step, chunk], {"ang": left})

    def gathered(step, to_right):
        if step < half - 1:
            return ALL_CHUNKS
        return FIRST_HALF if to_right else SECOND_HALF

    pos_edge = edge(0, pos_hbm.at[0], prev_pos_vmem, {"rows": below})
    amp_edge = edge(1, amp_hbm.at[0, 0], amp_ref.at[PREV], {"rows": below})
    started = [pos_edge, amp_edge]
    for step in range(half):
        for index in range(len(ALL_CHUNKS)):
            for to_right in (True, False):
                chunk = ALL_CHUNKS[index if to_right else -1 - index]
                if step > 0:
                    gather_copy(step - 1, chunk, to_right, coming=True).wait_recv()
                if chunk in gathered(step, to_right):
                    item = gather_copy(step, chunk, to_right)
                    item.start()
                    started.append(item)
        if step == 0:
            pos_edge.start()
            amp_edge.start()
        if step == 3:
            pos_edge.wait_recv()
            prev_load = pltpu.make_async_copy(prev_pos_vmem, prev_pos, load_sem.at[8])
            prev_load.start()
    for item in loads[2:]:
        item.wait()
    prev_load.wait()
    amp_edge.wait_recv()
    for to_right in (True, False):
        for chunk in gathered(half - 1, to_right):
            gather_copy(half - 1, chunk, to_right, coming=True).wait_recv()

    lane = lax.broadcasted_iota(jnp.int32, (TH, COLS), 1)
    cols, firsts, seconds, offsets, row_starts = [], [], [], [], []
    for slot in range(STRIPS):
        row = prev_pos[0, 0] if slot == PREV else pos_ref[0, 0, slot]
        col = prev_pos[1, 0] if slot == PREV else pos_ref[0, 1, slot]
        row_starts.append(jnp.clip(row, 0, TH if slot in (0, PREV) else TH - PIX))
        cols.append(jnp.clip(col, 0, blocks * COLS - PIX))
        spots = [place(cols[slot], shifts_ref[z, me], blocks) for z in range(LAYERS)]
        firsts.append([spot[0] for spot in spots])
        seconds.append([spot[1] for spot in spots])
        offsets.append([spot[2] for spot in spots])

    def strip(slot, chan):
        total = None
        for z in range(LAYERS):
            rows = pl.ds(chan * CHAN_ROWS, CHAN_ROWS)
            offset = offsets[slot][z]
            part0 = g_ref[firsts[slot][z], rows, :].astype(F32)[z * TH : (z + 1) * TH]
            part1 = g_ref[seconds[slot][z], rows, :].astype(F32)[z * TH : (z + 1) * TH]
            both = jnp.where(lane >= offset, part0, part1)
            value = pltpu.roll(both, (COLS - offset) & (COLS - 1), 1)
            total = value if total is None else total + value
        return total

    for chan in range(2):
        strip_prev[chan, TH:] = strip(PREV, chan)
        strip_prev[chan, :SHIFT] = jnp.zeros((SHIFT, COLS), F32)
        strip_own[chan, :TH] = strip(0, chan)
    lower = pl.ds(TH, PIX)
    upper = pl.ds(SHIFT, PIX)
    up_edge = edge(2, strip_prev.at[:, lower, :], strip_own.at[:, lower, :], {"rows": above})
    down_edge = edge(3, strip_own.at[:, upper, :], strip_prev.at[:, upper, :], {"rows": below})
    for item in (up_edge, down_edge):
        item.start()
        started.append(item)
    for slot in range(1, SLOTS):
        for chan in range(2):
            strip_ref[slot - 1, chan] = strip(slot, chan)

    probe_re = field_ref[0]
    probe_im = field_ref[1]
    depth = lax.broadcasted_iota(jnp.int32, (PIX, PIX), 0)

    def patch(slot, chan):
        rows = pl.ds(row_starts[slot], PIX)
        if slot == PREV:
            return strip_prev[chan, rows, :]
        if slot > 0:
            return strip_ref[slot - 1, chan, rows, :]
        value = strip_own[chan, rows, :]
        outside = (depth + row_starts[slot] >= TH) & (tile == tiles - 1)
        return jnp.where(outside, 0.0, value)

    def scans(slots):
        number = len(slots)
        exit_re, exit_im = [], []
        for slot in slots:
            damping = jnp.exp(-patch(slot, 1))
            sn, cs = sin_cos(patch(slot, 0))
            tre = damping * cs
            tim = damping * sn
            trans_ref[slot, 0] = tre
            trans_ref[slot, 1] = tim
            exit_re.append(probe_re * tre - probe_im * tim)
            exit_im.append(probe_re * tim + probe_im * tre)
        data = jnp.concatenate(
            [jnp.concatenate(exit_re, axis=1), jnp.concatenate(exit_im, axis=1)], axis=0
        )
        wide = left_product(m1h_ref[...], m1l_ref[...], data)
        wide = jnp.concatenate(
            [
                jnp.concatenate(
                    [wide[:PIX, j * PIX : (j + 1) * PIX], wide[PIX:, j * PIX : (j + 1) * PIX]],
                    axis=1,
                )
                for j in range(number)
            ],
            axis=0,
        )
        far = right_product(wide, m2h_ref[...], m2l_ref[...])
        residual = []
        for j, slot in enumerate(slots):
            rows = far[j * PIX : (j + 1) * PIX]
            re, im = rows[:, :PIX], rows[:, PIX:]
            live = tile > 0 if slot == PREV else slot < count_ref[0, 0]
            inverse = lax.rsqrt(jnp.maximum(re * re + im * im, AMP_FLOOR * AMP_FLOOR))
            factor = jnp.where(live, 1.0 - amp_ref[slot] * inverse, 0.0)
            residual.append(jnp.concatenate([re * factor, im * factor], axis=1))
        back = right_product(jnp.concatenate(residual, axis=0), m1h_ref[...], m1l_ref[...])
        tall = jnp.concatenate(
            [
                jnp.concatenate([back[j * PIX : (j + 1) * PIX, :PIX] for j in range(number)], axis=1),
                jnp.concatenate([back[j * PIX : (j + 1) * PIX, PIX:] for j in range(number)], axis=1),
            ],
            axis=0,
        )
        grad = left_product(m2h_ref[...], m2l_ref[...], tall)
        for j, slot in enumerate(slots):
            bre = grad[:PIX, j * PIX : (j + 1) * PIX]
            bim = grad[PIX:, j * PIX : (j + 1) * PIX]
            gre = probe_re * bre + probe_im * bim
            gim = probe_re * bim - probe_im * bre
            tre = trans_ref[slot, 0]
            tim = trans_ref[slot, 1]
            at = TH if slot == 0 else 0 if slot == PREV else SHIFT
            bottom = SHIFT if slot != PREV else TH + SHIFT
            start = (SHIFT if slot in range(1, SLOTS) else TH) - row_starts[slot]
            for chan, value in enumerate((tre * gim - tim * gre, -(tre * gre + tim * gim))):
                if at:
                    back_ref[slot, chan, :at] = jnp.zeros((at, PIX), F32)
                back_ref[slot, chan, at : at + PIX] = value
                back_ref[slot, chan, at + PIX : at + PIX + bottom] = jnp.zeros((bottom, PIX), F32)
                placed = back_ref[slot, chan, pl.ds(start, TH), :]
                for z in range(LAYERS):
                    first_row = chan * CHAN_ROWS + z * TH
                    rolled_ref[slot, first_row : first_row + TH] = pltpu.roll(
                        placed, offsets[slot][z], 1
                    )

    scans((1, 2, 3))
    up_edge.wait_recv()
    down_edge.wait_recv()
    scans((0, PREV))

    line = lax.broadcasted_iota(jnp.int32, (8, COLS), 1)

    def contribution(target, chunk):
        begin, size = CHUNKS[chunk]
        pieces = []
        for z_start in range(0, BLOCK_ROWS, TH):
            low, high = max(begin, z_start), min(begin + size, z_start + TH)
            if low >= high:
                continue
            z = (z_start // TH) % LAYERS
            total = None
            for slot in range(STRIPS):
                offset = offsets[slot][z]
                in_first = target == firsts[slot][z]
                in_second = target == seconds[slot][z]
                least = jnp.where(in_first, offset, jnp.where(in_second, 0, COLS))
                most = jnp.where(in_first, COLS, jnp.where(in_second, offset, 0))
                inside = (lane[: high - low] >= least) & (lane[: high - low] < most)
                value = jnp.where(inside, rolled_ref[slot, low:high], 0.0)
                total = value if total is None else total + value
            pieces.append(total)
        return jnp.concatenate(pieces, axis=0) if len(pieces) > 1 else pieces[0]

    def reduce_copy(step, chunk, to_right):
        rows = pl.ds(*CHUNKS[chunk])
        if to_right:
            return remote(
                out_r.at[step, rows, :],
                in_r.at[step, rows, :],
                send_r2.at[step, chunk],
                recv_r2.at[step, chunk],
                {"ang": right},
            )
        return remote(
            out_l.at[step, rows, :],
            in_l.at[step, rows, :],
            send_l2.at[step, chunk],
            recv_l2.at[step, chunk],
            {"ang": left},
        )

    def reduced(step, to_right):
        if step > 0:
            return ALL_CHUNKS
        return FIRST_HALF if to_right else SECOND_HALF

    def partial(step, chunk, to_right):
        rows = pl.ds(*CHUNKS[chunk])
        if to_right:
            target = lax.rem(me + half - step, blocks)
        else:
            target = lax.rem(me - half + step + blocks, blocks)
        value = contribution(target, chunk).astype(BF16)
        if step > 0 and chunk in reduced(step - 1, to_right):
            reduce_copy(step - 1, chunk, to_right).wait_recv()
            coming = in_r if to_right else in_l
            value = (value.astype(F32) + coming[step - 1, rows, :].astype(F32)).astype(BF16)
        going = out_r if to_right else out_l
        going[step, rows, :] = value

    for step in range(half):
        for index in range(len(ALL_CHUNKS)):
            ways = []
            for to_right in (True, False):
                chunk = ALL_CHUNKS[index if to_right else -1 - index]
                if chunk in reduced(step, to_right):
                    partial(step, chunk, to_right)
                    ways.append((chunk, to_right))
            for chunk, to_right in ways:
                item = reduce_copy(step, chunk, to_right)
                item.start()
                started.append(item)
    own = [
        contribution(me, chunk).astype(BF16).astype(F32) for chunk in ALL_CHUNKS
    ]
    for chunk in ALL_CHUNKS:
        for to_right in (True, False):
            reduce_copy(half - 1, chunk, to_right).wait_recv()
    own = jnp.concatenate(own, axis=0)
    for chan, ref in enumerate((delta_out, beta_out)):
        rows = pl.ds(chan * CHAN_ROWS, CHAN_ROWS)
        total = in_r[half - 1, rows, :].astype(F32) + in_l[half - 1, rows, :].astype(F32)
        total = total + own[chan * CHAN_ROWS : (chan + 1) * CHAN_ROWS]
        for z in range(LAYERS):
            ref[pl.ds(z, TH, stride=LAYERS), :] = total[z * TH : (z + 1) * TH]
    for item in started:
        item.wait_send()


VMEM = pl.BlockSpec(memory_space=pltpu.VMEM)
SMEM = pl.BlockSpec(memory_space=pltpu.SMEM)
HBM = pl.BlockSpec(memory_space=pltpu.HBM)


def on_device(delta_obj, beta_obj, layer_shifts, field, amplitudes, positions, counts):
    blocks = lax.axis_size("ang")
    tiles = lax.axis_size("rows")
    half = blocks // 2
    table = pltpu.VMEM((2 * PIX, 2 * PIX), BF16)
    stage = pltpu.VMEM((half, BLOCK_ROWS, COLS), BF16)
    ring_sems = pltpu.SemaphoreType.DMA((half, len(CHUNKS)))
    grad = jax.ShapeDtypeStruct((CHAN_ROWS, COLS), F32)
    pos = jnp.swapaxes(positions, 1, 2)
    delta_grad, beta_grad = pl.pallas_call(
        functools.partial(kernel, blocks, tiles),
        out_shape=(grad, grad),
        in_specs=[HBM] * 8 + [SMEM] * 3 + [HBM],
        out_specs=(VMEM, VMEM),
        scratch_shapes=[
            pltpu.VMEM((2, CHAN_ROWS, COLS), F32),
            pltpu.VMEM((2, PIX, PIX), F32),
            pltpu.VMEM((STRIPS, PIX, PIX), F32),
            table,
            table,
            table,
            table,
            pltpu.VMEM((2, SLOTS), jnp.int32),
            pltpu.SMEM((2, SLOTS), jnp.int32),
            pltpu.VMEM((blocks, BLOCK_ROWS, COLS), BF16),
            pltpu.VMEM((SLOTS - 1, 2, TH, PIX), F32),
            pltpu.VMEM((2, 2 * TH, PIX), F32),
            pltpu.VMEM((2, 2 * TH, PIX), F32),
            pltpu.VMEM((STRIPS, 2, PIX, PIX), F32),
            pltpu.VMEM((STRIPS, 2, 2 * TH, PIX), F32),
            pltpu.VMEM((STRIPS, BLOCK_ROWS, COLS), F32),
            stage,
            stage,
            stage,
            stage,
            pltpu.SemaphoreType.DMA((9,)),
            pltpu.SemaphoreType.DMA((4,)),
            pltpu.SemaphoreType.DMA((4,)),
        ]
        + [ring_sems] * 8,
        compiler_params=pltpu.CompilerParams(
            vmem_limit_bytes=67043328, collective_id=0, has_side_effects=True
        ),
    )(
        delta_obj.reshape(CHAN_ROWS, COLS),
        beta_obj.reshape(CHAN_ROWS, COLS),
        field,
        amplitudes,
        *dft_constants(),
        layer_shifts.T,
        pos,
        counts,
        pos,
    )
    shape = (TH, LAYERS, COLS)
    return (delta_grad.reshape(shape), beta_grad.reshape(shape))


def solution(mesh):
    placed = (
        P("rows", None, "ang"),
        P("rows", None, "ang"),
        P(),
        P(),
        P("ang", "rows", None, None),
        P("ang", "rows", None),
        P("ang", "rows"),
    )
    return jax.shard_map(
        on_device,
        mesh=mesh,
        in_specs=placed,
        out_specs=(P("rows", None, "ang"), P("rows", None, "ang")),
        check_vma=False,
    )
```

time: 165 us -> 72.2 us (0.44)
  waiting for transfers between devices: 128 us -> 0 us
  Pallas kernels: 6.46 us -> 68.4 us
  between operations: 14.8 us -> 1.3 us
  starting transfers between devices: 7.55 us -> 0 us
  local copies, waits for them, and re-layouts: 6.91 us -> 2.27 us
    pallas_call x3 -> x1, Pallas kernels: 6.46 us -> 68.4 us  [on_device(): pl.pallas_call(functools.partial(kernel, blocks, tiles), out_shape=(grad,...]
    all_gather x1 -> x0, waiting for transfers between devices: 60.7 us -> none  [on_device(): gathered = lax.all_gather(own, 'ang')]
    reduce_scatter x1 -> x0, waiting for transfers between devices: 56.2 us -> none  [on_device(): total = lax.psum_scatter(spread, 'ang', scatter_dimension=0)]
    ppermute x3 -> x0, waiting for transfers between devices: 10.9 us -> none  [shift_rows(): lax.ppermute(value, 'rows', [(i, i + steps) for i in range(first, last)])]
    ppermute x3 -> x0, starting transfers between devices: 7.48 us -> none  [shift_rows(): lax.ppermute(value, 'rows', [(i, i + steps) for i in range(first, last)])]
    unnamed x22 -> x4, local copies, waits for them, and re-layouts: 4.36 us -> 2.27 us
  transfers between devices with their start and end apart: 5 -> 0, of which waited for: 5 -> 0; matrix products, arithmetic and copies ran while one was open for 1% -> 0% of each run, Pallas kernels for 0% -> 0%
where the time goes in v2:
time: 72.2 us; the launch traced here: 72 us
  Pallas kernels  68.4 us (95%)
  local copies, waits for them, and re-layouts  2.27 us (3%)
  between operations  1.3 us (2%)
    pallas_call x1, Pallas kernels, on_device(): pl.pallas_call(functools.partial(kernel, blocks, tiles), out_shape=(grad,...  68.4 us
    unnamed x4, local copies, waits for them, and re-layouts  2.27 us

profile of v2, /device:TPU:6, one launch (start us, length us, event | category | flops | bytes accessed | tf_op | source)
XLA Modules:
  0.0 72.0 jit_solution(3039969379613240657)
XLA Ops:
  1.3 68.4 %shard_map.122 = (f32[272,128]{1,0:T(8,128)}, f32[272,128]{1,0:T(8,128)}) custom-call(f32[272,128]{1,0:T(8,128)} %bitcast.6, f32[272,128]{1,0:T(8,128)} %bitcast.7, f32[2,128,128]{2,1,0:T(8,128)} %field_hbm.1, f32[1,4,128,128]{3,2,1,0:T(8,128)} %amp_hbm.1, bf16[256,256]{1,0:T(8,128)(2,1)} %constant.8.clone.m1h_hbm, bf16[256,256]{1,0:T(8,128)(2,1)} %constant.9.clone.m1l_hbm, ...), custom_call_target="tpu_custom_call" | custom-call | tf_op jit(solution)/shard_map/pallas_call | solution.py:463
  69.7 0.0 copy-start
  69.7 1.6 %copy.16 = f32[136,2,128]{2,1,0:T(2,128)} copy(f32[136,2,128]{2,1,0:T(2,128)} %bitcast.9) | data formatting | bytes 278528
  71.3 0.0 copy-done
  71.3 0.7 copy.17
Async XLA Ops:
  69.7 1.6 %copy-start = (f32[272,128]{1,0:T(8,128)S(1)}, f32[272,128]{1,0:T(8,128)}, u32[]{:S(2)}) copy-start(f32[272,128]{1,0:T(8,128)} %get-tuple-element.5) | copy-start | bytes 417796

commit v3 on v2

--- a/solution.py
+++ b/solution.py
@@ -87,10 +87,21 @@
     return first, second, offset
 
 
-CHUNKS = ((0, 144), (144, 128), (272, 144), (416, 128))
-FIRST_HALF = (0, 1)
-SECOND_HALF = (2, 3)
-ALL_CHUNKS = (0, 1, 2, 3)
+PARTS = (144, 128)
+
+
+def chunk_table():
+    table, start = [], 0
+    for size in PARTS * 2:
+        table.append((start, size))
+        start += size
+    return tuple(table)
+
+
+CHUNKS = chunk_table()
+ALL_CHUNKS = tuple(range(len(CHUNKS)))
+FIRST_HALF = ALL_CHUNKS[: len(PARTS)]
+SECOND_HALF = ALL_CHUNKS[len(PARTS) :]
 STRIPS = SLOTS + 1
 PREV = SLOTS
 
@@ -106,12 +117,10 @@
     m1l_hbm,
     m2h_hbm,
     m2l_hbm,
-    shifts_ref,
-    pos_ref,
-    count_ref,
+    shifts_hbm,
     pos_hbm,
-    delta_out,
-    beta_out,
+    count_hbm,
+    out_ref,
     object_ref,
     field_ref,
     amp_ref,
@@ -119,6 +128,9 @@
     m1l_ref,
     m2h_ref,
     m2l_ref,
+    shifts_ref,
+    pos_ref,
+    count_ref,
     prev_pos_vmem,
     prev_pos,
     g_ref,
@@ -143,6 +155,7 @@
     recv_r2,
     send_l2,
     recv_l2,
+    ready_ref,
 ):
     me = lax.axis_index("ang")
     right = lax.rem(me + 1, blocks)
@@ -164,6 +177,9 @@
                 (m1l_hbm, m1l_ref),
                 (m2h_hbm, m2h_ref),
                 (m2l_hbm, m2l_ref),
+                (shifts_hbm, shifts_ref),
+                (pos_hbm, pos_ref),
+                (count_hbm, count_ref),
             )
         )
     ]
@@ -223,7 +239,7 @@
             amp_edge.start()
         if step == 3:
             pos_edge.wait_recv()
-            prev_load = pltpu.make_async_copy(prev_pos_vmem, prev_pos, load_sem.at[8])
+            prev_load = pltpu.make_async_copy(prev_pos_vmem, prev_pos, load_sem.at[11])
             prev_load.start()
     for item in loads[2:]:
         item.wait()
@@ -257,17 +273,24 @@
             total = value if total is None else total + value
         return total
 
+    lower = pl.ds(TH, PIX)
+    upper = pl.ds(SHIFT, PIX)
+    strip_edges = []
     for chan in range(2):
         strip_prev[chan, TH:] = strip(PREV, chan)
         strip_prev[chan, :SHIFT] = jnp.zeros((SHIFT, COLS), F32)
         strip_own[chan, :TH] = strip(0, chan)
-    lower = pl.ds(TH, PIX)
-    upper = pl.ds(SHIFT, PIX)
-    up_edge = edge(2, strip_prev.at[:, lower, :], strip_own.at[:, lower, :], {"rows": above})
-    down_edge = edge(3, strip_own.at[:, upper, :], strip_prev.at[:, upper, :], {"rows": below})
-    for item in (up_edge, down_edge):
-        item.start()
-        started.append(item)
+        strip_edges += [
+            edge(
+                2 + chan, strip_prev.at[chan, lower, :], strip_own.at[chan, lower, :], {"rows": above}
+            ),
+            edge(
+                4 + chan, strip_own.at[chan, upper, :], strip_prev.at[chan, upper, :], {"rows": below}
+            ),
+        ]
+        for item in strip_edges[-2:]:
+            item.start()
+    started += strip_edges
     for slot in range(1, SLOTS):
         for chan in range(2):
             strip_ref[slot - 1, chan] = strip(slot, chan)
@@ -353,8 +376,8 @@
                     )
 
     scans((1, 2, 3))
-    up_edge.wait_recv()
-    down_edge.wait_recv()
+    for item in strip_edges:
+        item.wait_recv()
     scans((0, PREV))
 
     line = lax.broadcasted_iota(jnp.int32, (8, COLS), 1)
@@ -403,51 +426,58 @@
             return ALL_CHUNKS
         return FIRST_HALF if to_right else SECOND_HALF
 
-    def partial(step, chunk, to_right):
-        rows = pl.ds(*CHUNKS[chunk])
+    def prepare(step, chunk, to_right):
         if to_right:
             target = lax.rem(me + half - step, blocks)
         else:
             target = lax.rem(me - half + step + blocks, blocks)
-        value = contribution(target, chunk).astype(BF16)
+        way = 0 if to_right else 1
+        ready_ref[step % 2, way, pl.ds(*CHUNKS[chunk]), :] = contribution(target, chunk)
+
+    def advance(step, chunk, to_right):
+        rows = pl.ds(*CHUNKS[chunk])
+        going, coming = (out_r, in_r) if to_right else (out_l, in_l)
+        total = ready_ref[step % 2, 0 if to_right else 1, rows, :]
         if step > 0 and chunk in reduced(step - 1, to_right):
             reduce_copy(step - 1, chunk, to_right).wait_recv()
-            coming = in_r if to_right else in_l
-            value = (value.astype(F32) + coming[step - 1, rows, :].astype(F32)).astype(BF16)
-        going = out_r if to_right else out_l
-        going[step, rows, :] = value
-
+            total = total + coming[step - 1, rows, :].astype(F32)
+        going[step, rows, :] = total.astype(BF16)
+        item = reduce_copy(step, chunk, to_right)
+        item.start()
+        started.append(item)
+
+    own = []
     for step in range(half):
         for index in range(len(ALL_CHUNKS)):
-            ways = []
             for to_right in (True, False):
                 chunk = ALL_CHUNKS[index if to_right else -1 - index]
                 if chunk in reduced(step, to_right):
-                    partial(step, chunk, to_right)
-                    ways.append((chunk, to_right))
-            for chunk, to_right in ways:
-                item = reduce_copy(step, chunk, to_right)
-                item.start()
-                started.append(item)
-    own = [
-        contribution(me, chunk).astype(BF16).astype(F32) for chunk in ALL_CHUNKS
-    ]
+                    if step == 0:
+                        prepare(step, chunk, to_right)
+                    advance(step, chunk, to_right)
+                if step > 0 and step + 1 < half:
+                    prepare(step + 1, chunk, to_right)
+            if step == half - 1:
+                own.append(contribution(me, ALL_CHUNKS[index]))
+        if step == 0:
+            for index in range(len(ALL_CHUNKS)):
+                for to_right in (True, False):
+                    prepare(1, ALL_CHUNKS[index if to_right else -1 - index], to_right)
     for chunk in ALL_CHUNKS:
         for to_right in (True, False):
             reduce_copy(half - 1, chunk, to_right).wait_recv()
     own = jnp.concatenate(own, axis=0)
-    for chan, ref in enumerate((delta_out, beta_out)):
+    for chan in range(2):
         rows = pl.ds(chan * CHAN_ROWS, CHAN_ROWS)
         total = in_r[half - 1, rows, :].astype(F32) + in_l[half - 1, rows, :].astype(F32)
         total = total + own[chan * CHAN_ROWS : (chan + 1) * CHAN_ROWS]
         for z in range(LAYERS):
-            ref[pl.ds(z, TH, stride=LAYERS), :] = total[z * TH : (z + 1) * TH]
+            out_ref[chan, pl.ds(z, TH, stride=LAYERS), :] = total[z * TH : (z + 1) * TH]
     for item in started:
         item.wait_send()
 
 
 VMEM = pl.BlockSpec(memory_space=pltpu.VMEM)
-SMEM = pl.BlockSpec(memory_space=pltpu.SMEM)
 HBM = pl.BlockSpec(memory_space=pltpu.HBM)
 
 
@@ -458,13 +488,12 @@
     table = pltpu.VMEM((2 * PIX, 2 * PIX), BF16)
     stage = pltpu.VMEM((half, BLOCK_ROWS, COLS), BF16)
     ring_sems = pltpu.SemaphoreType.DMA((half, len(CHUNKS)))
-    grad = jax.ShapeDtypeStruct((CHAN_ROWS, COLS), F32)
     pos = jnp.swapaxes(positions, 1, 2)
-    delta_grad, beta_grad = pl.pallas_call(
+    grad = pl.pallas_call(
         functools.partial(kernel, blocks, tiles),
-        out_shape=(grad, grad),
-        in_specs=[HBM] * 8 + [SMEM] * 3 + [HBM],
-        out_specs=(VMEM, VMEM),
+        out_shape=jax.ShapeDtypeStruct((2, CHAN_ROWS, COLS), F32),
+        in_specs=[HBM] * 11,
+        out_specs=VMEM,
         scratch_shapes=[
             pltpu.VMEM((2, CHAN_ROWS, COLS), F32),
             pltpu.VMEM((2, PIX, PIX), F32),
@@ -473,6 +502,9 @@
             table,
             table,
             table,
+            pltpu.SMEM((LAYERS, blocks), jnp.int32),
+            pltpu.SMEM((1, 2, SLOTS), jnp.int32),
+            pltpu.SMEM((1, 1), jnp.int32),
             pltpu.VMEM((2, SLOTS), jnp.int32),
             pltpu.SMEM((2, SLOTS), jnp.int32),
             pltpu.VMEM((blocks, BLOCK_ROWS, COLS), BF16),
@@ -486,11 +518,12 @@
             stage,
             stage,
             stage,
-            pltpu.SemaphoreType.DMA((9,)),
-            pltpu.SemaphoreType.DMA((4,)),
-            pltpu.SemaphoreType.DMA((4,)),
+            pltpu.SemaphoreType.DMA((12,)),
+            pltpu.SemaphoreType.DMA((6,)),
+            pltpu.SemaphoreType.DMA((6,)),
         ]
-        + [ring_sems] * 8,
+        + [ring_sems] * 8
+        + [pltpu.VMEM((2, 2, BLOCK_ROWS, COLS), F32)],
         compiler_params=pltpu.CompilerParams(
             vmem_limit_bytes=67043328, collective_id=0, has_side_effects=True
         ),
@@ -503,10 +536,9 @@
         layer_shifts.T,
         pos,
         counts,
-        pos,
     )
     shape = (TH, LAYERS, COLS)
-    return (delta_grad.reshape(shape), beta_grad.reshape(shape))
+    return (grad[0].reshape(shape), grad[1].reshape(shape))
 
 
 def solution(mesh):

time: 72.2 us -> 68.8 us (0.953)
  Pallas kernels: 68.4 us -> 65.6 us
    pallas_call x1, Pallas kernels: 68.4 us -> 65.6 us  [on_device(): pl.pallas_call(functools.partial(kernel, blocks, tiles), out_shape=jax.Sh...]
    unnamed x4 -> x0, local copies, waits for them, and re-layouts: 2.27 us -> none
    slice x0 -> x1, local copies, waits for them, and re-layouts: none -> 1.7 us  [on_device(): return (grad[0].reshape(shape), grad[1].reshape(shape))]
where the time goes in v3:
time: 68.8 us; the launch traced here: 68.6 us
  Pallas kernels  65.6 us (95%)
  local copies, waits for them, and re-layouts  1.7 us (2%)
  between operations  1.29 us (2%)
    pallas_call x1, Pallas kernels, on_device(): pl.pallas_call(functools.partial(kernel, blocks, tiles), out_shape=jax.Sh...  65.6 us
    slice x1, local copies, waits for them, and re-layouts, on_device(): return (grad[0].reshape(shape), grad[1].reshape(shape))  1.7 us

profile of v3, /device:TPU:6, one launch (start us, length us, event | category | flops | bytes accessed | tf_op | source)
XLA Modules:
  0.0 68.6 jit_solution(10032456657895163977)
XLA Ops:
  1.3 65.6 %shard_map.122 = f32[2,272,128]{2,1,0:T(8,128)} custom-call(f32[272,128]{1,0:T(8,128)} %bitcast.8, f32[272,128]{1,0:T(8,128)} %bitcast.9, f32[2,128,128]{2,1,0:T(8,128)} %field_hbm.1, f32[1,4,128,128]{3,2,1,0:T(8,128)} %amp_hbm.1, bf16[256,256]{1,0:T(8,128)(2,1)} %constant.8.clone.m1h_hbm, bf16[256,256]{1,0:T(8,128)(2,1)} %constant.9.clone.m1l_hbm, ...), custom_call_target="tpu_custom_call" | custom-call | tf_op jit(solution)/shard_map/pallas_call | solution.py:492
  66.9 1.7 %fusion = (f32[1,272,128]{2,1,0:T(8,128)}, f32[1,272,128]{2,1,0:T(8,128)}) fusion(f32[2,272,128]{2,1,0:T(8,128)} %shard_map.122), kind=kLoop, calls=%fused_computation | loop fusion | bytes 557056 | tf_op jit(solution)/shard_map/slice | solution.py:541

commit v4 on v3

--- a/solution.py
+++ b/solution.py
@@ -156,6 +156,8 @@
     send_l2,
     recv_l2,
     ready_ref,
+    edge_out,
+    edge_in,
 ):
     me = lax.axis_index("ang")
     right = lax.rem(me + 1, blocks)
@@ -280,13 +282,11 @@
         strip_prev[chan, TH:] = strip(PREV, chan)
         strip_prev[chan, :SHIFT] = jnp.zeros((SHIFT, COLS), F32)
         strip_own[chan, :TH] = strip(0, chan)
+        edge_out[chan, 0] = strip_prev[chan, lower, :].astype(BF16)
+        edge_out[chan, 1] = strip_own[chan, upper, :].astype(BF16)
         strip_edges += [
-            edge(
-                2 + chan, strip_prev.at[chan, lower, :], strip_own.at[chan, lower, :], {"rows": above}
-            ),
-            edge(
-                4 + chan, strip_own.at[chan, upper, :], strip_prev.at[chan, upper, :], {"rows": below}
-            ),
+            edge(2 + chan, edge_out.at[chan, 0], edge_in.at[chan, 0], {"rows": above}),
+            edge(4 + chan, edge_out.at[chan, 1], edge_in.at[chan, 1], {"rows": below}),
         ]
         for item in strip_edges[-2:]:
             item.start()
@@ -375,10 +375,12 @@
                         placed, offsets[slot][z], 1
                     )
 
-    scans((1, 2, 3))
     for item in strip_edges:
         item.wait_recv()
-    scans((0, PREV))
+    for chan in range(2):
+        strip_own[chan, lower, :] = edge_in[chan, 0].astype(F32)
+        strip_prev[chan, upper, :] = edge_in[chan, 1].astype(F32)
+    scans((1, 2, 3, 0, PREV))
 
     line = lax.broadcasted_iota(jnp.int32, (8, COLS), 1)
 
@@ -523,18 +525,24 @@
             pltpu.SemaphoreType.DMA((6,)),
         ]
         + [ring_sems] * 8
-        + [pltpu.VMEM((2, 2, BLOCK_ROWS, COLS), F32)],
+        + [pltpu.VMEM((2, 2, BLOCK_ROWS, COLS), F32)]
+        + [pltpu.VMEM((2, 2, PIX, PIX), BF16)] * 2,
         compiler_params=pltpu.CompilerParams(
-            vmem_limit_bytes=67043328, collective_id=0, has_side_effects=True
+            vmem_limit_bytes=50331648, collective_id=0, has_side_effects=True
         ),
     )(
-        delta_obj.reshape(CHAN_ROWS, COLS),
-        beta_obj.reshape(CHAN_ROWS, COLS),
-        field,
-        amplitudes,
-        *dft_constants(),
-        layer_shifts.T,
-        pos,
+        *(
+            pltpu.with_memory_space_constraint(value, pltpu.HBM)
+            for value in (
+                delta_obj.reshape(CHAN_ROWS, COLS),
+                beta_obj.reshape(CHAN_ROWS, COLS),
+                field,
+                amplitudes,
+                *(jnp.asarray(m) for m in dft_constants()),
+                layer_shifts.T,
+                pos,
+            )
+        ),
         counts,
     )
     shape = (TH, LAYERS, COLS)

time: 68.8 us -> 67 us (0.974)
  Pallas kernels: 65.6 us -> 64.3 us
  local copies, waits for them, and re-layouts: 1.7 us -> 0.72 us
    pallas_call x1, Pallas kernels: 65.6 us -> 64.3 us  [on_device(): pl.pallas_call(functools.partial(kernel, blocks, tiles), out_shape=jax.Sh...]
    slice x1, local copies, waits for them, and re-layouts: 1.7 us -> 0.72 us  [on_device(): return (grad[0].reshape(shape), grad[1].reshape(shape))]
where the time goes in v4:
time: 67 us; the launch traced here: 66.3 us
  Pallas kernels  64.3 us (96%)
  between operations  1.29 us (2%)
  local copies, waits for them, and re-layouts  0.72 us (1%)
    pallas_call x1, Pallas kernels, on_device(): pl.pallas_call(functools.partial(kernel, blocks, tiles), out_shape=jax.Sh...  64.3 us

profile of v4, /device:TPU:6, one launch (start us, length us, event | category | flops | bytes accessed | tf_op | source)
XLA Modules:
  0.0 66.3 jit_solution(7178561370089997011)
XLA Ops:
  1.3 64.3 %shard_map.122 = f32[2,272,128]{2,1,0:T(8,128)S(1)} custom-call(f32[272,128]{1,0:T(8,128)} %bitcast.8, f32[272,128]{1,0:T(8,128)} %bitcast.9, f32[2,128,128]{2,1,0:T(8,128)} %field_hbm.1, f32[1,4,128,128]{3,2,1,0:T(8,128)} %amp_hbm.1, bf16[256,256]{1,0:T(8,128)(2,1)} %constant.8.clone.m1h_hbm, bf16[256,256]{1,0:T(8,128)(2,1)} %constant.9.clone.m1l_hbm, ...), custom_call_target="tpu_custom_call" | custom-call | tf_op jit(solution)/shard_map/pallas_call | solution.py:494
  65.6 0.7 %fusion = (f32[1,272,128]{2,1,0:T(8,128)}, f32[1,272,128]{2,1,0:T(8,128)}) fusion(f32[2,272,128]{2,1,0:T(8,128)S(1)} %shard_map.122), kind=kLoop, calls=%fused_computation | loop fusion | bytes 557056 | tf_op jit(solution)/shard_map/slice | solution.py:549

commit v5 on v4

--- a/solution.py
+++ b/solution.py
@@ -375,12 +375,25 @@
                         placed, offsets[slot][z], 1
                     )
 
-    for item in strip_edges:
-        item.wait_recv()
-    for chan in range(2):
-        strip_own[chan, lower, :] = edge_in[chan, 0].astype(F32)
-        strip_prev[chan, upper, :] = edge_in[chan, 1].astype(F32)
-    scans((1, 2, 3, 0, PREV))
+    def receive_strips():
+        for item in strip_edges:
+            item.wait_recv()
+        for chan in range(2):
+            strip_own[chan, lower, :] = edge_in[chan, 0].astype(F32)
+            strip_prev[chan, upper, :] = edge_in[chan, 1].astype(F32)
+
+    far_strip = lax.rem(tile, 2) == 1
+
+    @pl.when(far_strip)
+    def _():
+        scans((1, 2, 3))
+        receive_strips()
+        scans((0, PREV))
+
+    @pl.when(jnp.logical_not(far_strip))
+    def _():
+        receive_strips()
+        scans((1, 2, 3, 0, PREV))
 
     line = lax.broadcasted_iota(jnp.int32, (8, COLS), 1)
 

time: 67 us -> 66.8 us (level)
  no operation moved by 1% of the time
where the time goes in v5:
time: 66.8 us; the launch traced here: 66.2 us
  Pallas kernels  64.2 us (96%)
  between operations  1.29 us (2%)
  local copies, waits for them, and re-layouts  0.72 us (1%)
    pallas_call x1, Pallas kernels, on_device(): pl.pallas_call(functools.partial(kernel, blocks, tiles), out_shape=jax.Sh...  64.2 us

profile of v5, /device:TPU:6, one launch (start us, length us, event | category | flops | bytes accessed | tf_op | source)
XLA Modules:
  0.0 66.2 jit_solution(3506723279080624970)
XLA Ops:
  1.3 64.2 %shard_map.122 = f32[2,272,128]{2,1,0:T(8,128)S(1)} custom-call(f32[272,128]{1,0:T(8,128)} %bitcast.8, f32[272,128]{1,0:T(8,128)} %bitcast.9, f32[2,128,128]{2,1,0:T(8,128)} %field_hbm.1, f32[1,4,128,128]{3,2,1,0:T(8,128)} %amp_hbm.1, bf16[256,256]{1,0:T(8,128)(2,1)} %constant.8.clone.m1h_hbm, bf16[256,256]{1,0:T(8,128)(2,1)} %constant.9.clone.m1l_hbm, ...), custom_call_target="tpu_custom_call" | custom-call | tf_op jit(solution)/shard_map/pallas_call | solution.py:507
  65.5 0.7 %fusion = (f32[1,272,128]{2,1,0:T(8,128)}, f32[1,272,128]{2,1,0:T(8,128)}) fusion(f32[2,272,128]{2,1,0:T(8,128)S(1)} %shard_map.122), kind=kLoop, calls=%fused_computation | loop fusion | bytes 557056 | tf_op jit(solution)/shard_map/slice | solution.py:562

commit v6 on v5

--- a/solution.py
+++ b/solution.py
@@ -185,7 +185,7 @@
             )
         )
     ]
-    for item in loads:
+    for item in loads[:2]:
         item.start()
     barrier = pltpu.get_barrier_semaphore()
     for target in ({"ang": left}, {"ang": right}, {"rows": above}, {"rows": below}):
@@ -237,6 +237,8 @@
                     item.start()
                     started.append(item)
         if step == 0:
+            for item in loads[2:]:
+                item.start()
             pos_edge.start()
             amp_edge.start()
         if step == 3:
@@ -478,11 +480,11 @@
             for index in range(len(ALL_CHUNKS)):
                 for to_right in (True, False):
                     prepare(1, ALL_CHUNKS[index if to_right else -1 - index], to_right)
-    for chunk in ALL_CHUNKS:
-        for to_right in (True, False):
-            reduce_copy(half - 1, chunk, to_right).wait_recv()
     own = jnp.concatenate(own, axis=0)
-    for chan in range(2):
+    for chan, chunks in ((0, FIRST_HALF), (1, SECOND_HALF)):
+        for chunk in chunks:
+            for to_right in (True, False):
+                reduce_copy(half - 1, chunk, to_right).wait_recv()
         rows = pl.ds(chan * CHAN_ROWS, CHAN_ROWS)
         total = in_r[half - 1, rows, :].astype(F32) + in_l[half - 1, rows, :].astype(F32)
         total = total + own[chan * CHAN_ROWS : (chan + 1) * CHAN_ROWS]

time: 66.8 us -> 66.8 us (level)
  no operation moved by 1% of the time
where the time goes in v6:
time: 66.8 us; the launch traced here: 66.3 us
  Pallas kernels  64.2 us (96%)
  between operations  1.29 us (2%)
  local copies, waits for them, and re-layouts  0.72 us (1%)
    pallas_call x1, Pallas kernels, on_device(): pl.pallas_call(functools.partial(kernel, blocks, tiles), out_shape=jax.Sh...  64.2 us

profile of v6, /device:TPU:6, one launch (start us, length us, event | category | flops | bytes accessed | tf_op | source)
XLA Modules:
  0.0 66.3 jit_solution(18049928759519798255)
XLA Ops:
  1.3 64.2 %shard_map.122 = f32[2,272,128]{2,1,0:T(8,128)S(1)} custom-call(f32[272,128]{1,0:T(8,128)} %bitcast.8, f32[272,128]{1,0:T(8,128)} %bitcast.9, f32[2,128,128]{2,1,0:T(8,128)} %field_hbm.1, f32[1,4,128,128]{3,2,1,0:T(8,128)} %amp_hbm.1, bf16[256,256]{1,0:T(8,128)(2,1)} %constant.8.clone.m1h_hbm, bf16[256,256]{1,0:T(8,128)(2,1)} %constant.9.clone.m1l_hbm, ...), custom_call_target="tpu_custom_call" | custom-call | tf_op jit(solution)/shard_map/pallas_call | solution.py:509
  65.5 0.7 %fusion = (f32[1,272,128]{2,1,0:T(8,128)}, f32[1,272,128]{2,1,0:T(8,128)}) fusion(f32[2,272,128]{2,1,0:T(8,128)S(1)} %shard_map.122), kind=kLoop, calls=%fused_computation | loop fusion | bytes 557056 | tf_op jit(solution)/shard_map/slice | solution.py:564
